TPU v7x, 32 devices: a whole 2x2x4 slice. The times are simulated.
32 devices in a mesh: rep: 2 (over x), shard: 16 (over z, y, core).
Axes of the slice: x: 2, y: 2, z: 4, core: 2. Of those that a mesh axis runs over, the one named last changes fastest.
Arguments:
- block_input: bfloat16 [4096, 2048], P(('rep', 'shard')), may hold values from -6 to 6
- out_grad: bfloat16 [4096, 2048], P(('rep', 'shard')), may hold values from -6 to 6
- segments: int32 [32, 128], P(('rep', 'shard')), may hold values from 0 to 2, as said below
- positions: int32 [32, 128], P(('rep', 'shard')), may hold values from 0 to 1023, as said below
- attn_gain: float32 [2048], replicated, may hold values from 0.5 to 1.5
- mlp_gain: float32 [2048], replicated, may hold values from 0.5 to 1.5
- q_gain: float32 [128], replicated, may hold values from 0.5 to 2
- k_gain: float32 [128], replicated, may hold values from 0.5 to 2
- w_q: bfloat16 [2048, 2048], P('shard'), may hold values from -0.125 to 0.125
- key_matrix: bfloat16 [2048, 1024], P('shard'), may hold values from -0.125 to 0.125
- value_matrix: bfloat16 [2048, 1024], P('shard'), may hold values from -0.125 to 0.125
- w_o: bfloat16 [2048, 2048], P('shard'), may hold values from -0.75 to 0.75
- w_gate: bfloat16 [2048, 6144], P('shard'), may hold values from -0.125 to 0.125
- w_up: bfloat16 [2048, 6144], P('shard'), may hold values from -0.125 to 0.125
- w_down: bfloat16 [2048, 6144], P('shard'), may hold values from -0.078125 to 0.078125
Outputs:
- output: bfloat16 [4096, 2048], P(('rep', 'shard'))
- grad_input: float32 [4096, 2048], P(('rep', 'shard'))
- grad_w_q: float32 [2048, 2048], P('shard')
- grad_w_k: float32 [2048, 1024], P('shard')
- grad_w_v: float32 [2048, 1024], P('shard')
- grad_w_o: float32 [2048, 2048], P('shard')
- grad_w_gate: float32 [2048, 6144], P('shard')
- grad_w_up: float32 [2048, 6144], P('shard')
- grad_w_down: float32 [2048, 6144], P('shard')
- grad_attn_gain: float32 [2048], replicated
- grad_mlp_gain: float32 [2048], replicated
- grad_q_gain: float32 [128], replicated
- grad_k_gain: float32 [128], replicated
Inputs may be any that keep to these rules, and one draw needn't show every extreme that they name: `segments`: in each sequence the segment numbers never fall, the first token has 0 and the last has 2. Within a segment the positions rise by one from token to token; segments 1 and 2 start at position 0.
All inputs are finite; a program needn't handle non-finite values.
Results may differ from a plain program's by a relative error of at most 0.015.
Values may be sent and summed in bfloat16 or wider, within the bound.
No kernel may reach another device: no remote copies, remote signals or barrier semaphores. Data moves between devices by JAX's collectives and lax.ppermute only.
A program may use at most 768 MiB of HBM per device.

v0:
```python
import math
import jax
import jax.numpy as jnp
from jax import lax
from jax.sharding import PartitionSpec as P

EPSILON = 1e-06
ROPE_BASE = 1000000.0
NEG_FILL = -1e30


def rope_tables(positions, half):
    freq = jnp.exp(jnp.arange(half, dtype=jnp.float32) * (-math.log(ROPE_BASE) / half))
    angles = positions.reshape(-1).astype(jnp.float32)[:, None, None] * freq
    return (jnp.cos(angles), jnp.sin(angles))


def rotate(vectors, cosine, sine):
    half = vectors.shape[-1] // 2
    first, second = (vectors[..., :half], vectors[..., half:])
    return jnp.concatenate([first * cosine - second * sine, second * cosine + first * sine], -1)


def unrotate(grads, cosine, sine):
    half = grads.shape[-1] // 2
    first, second = (grads[..., :half], grads[..., half:])
    return jnp.concatenate([first * cosine + second * sine, second * cosine - first * sine], -1)


def head_norm(heads, gain):
    recip = lax.rsqrt(jnp.mean(heads * heads, -1, keepdims=True) + EPSILON)
    return (heads * recip * gain, recip)


def norm_back(grads, inputs, recip, gain, axes):
    normal = inputs * recip
    scaled = grads * gain
    gain_grad = jnp.sum(grads * normal, axis=axes)
    input_grad = recip * (scaled - normal * jnp.mean(scaled * normal, -1, keepdims=True))
    return (input_grad, gain_grad)


def attention_mask(segments):
    packed_length = segments.shape[1]
    same = segments[:, :, None] == segments[:, None, :]
    places = jnp.arange(packed_length)
    causal = places[None, :] <= places[:, None]
    return same & causal[None]


def contract_rows(left, right):
    return lax.dot_general(
        left, right, (((0,), (0,)), ((), ())), preferred_element_type=jnp.float32
    )


def contract_cols(left, right):
    return lax.dot_general(
        left, right, (((1,), (1,)), ((), ())), preferred_element_type=jnp.float32
    )


def head_scores(rotated_query_rows, rotated_key_rows, mask, kv_heads, head):
    sequence_list, packed_length = (mask.shape[0], mask.shape[1])
    groups = rotated_query_rows.shape[1] // kv_heads
    query_rows = rotated_query_rows.reshape(sequence_list, packed_length, kv_heads, groups, head)
    every_key_row = rotated_key_rows.reshape(sequence_list, packed_length, kv_heads, head)
    scores = jnp.einsum(
        "slkgd,smkd->skglm", query_rows, every_key_row, preferred_element_type=jnp.float32
    ) * head ** (-0.5)
    return (jnp.where(mask[:, None, None], scores, NEG_FILL), query_rows, every_key_row)


def attend_forward(rotated_query_rows, rotated_key_rows, value_rows, mask):
    sequence_list, packed_length = (mask.shape[0], mask.shape[1])
    kv_heads, head = (value_rows.shape[1], value_rows.shape[2])
    scores, query_rows, every_key_row = head_scores(
        rotated_query_rows, rotated_key_rows, mask, kv_heads, head
    )
    top = jnp.max(scores, -1, keepdims=True)
    expo = jnp.exp(scores - top)
    total = jnp.sum(expo, -1, keepdims=True)
    probs = (expo / total).astype(jnp.bfloat16)
    log_total = top + jnp.log(total)
    value_heads = value_rows.reshape(sequence_list, packed_length, kv_heads, head)
    attended_rows = jnp.einsum(
        "skglm,smkd->slkgd", probs, value_heads, preferred_element_type=jnp.float32
    )
    return (
        attended_rows.reshape(
            sequence_list * packed_length, rotated_query_rows.shape[1] * head
        ).astype(jnp.bfloat16),
        log_total,
    )


def attend_backward(
    rotated_query_rows,
    rotated_key_rows,
    value_rows,
    attended_rows,
    attended_gradient,
    log_total,
    mask,
):
    sequence_list, packed_length = (mask.shape[0], mask.shape[1])
    kv_heads, head = (value_rows.shape[1], value_rows.shape[2])
    groups = rotated_query_rows.shape[1] // kv_heads
    scores, query_rows, every_key_row = head_scores(
        rotated_query_rows, rotated_key_rows, mask, kv_heads, head
    )
    probs_back = jnp.where(mask[:, None, None], jnp.exp(scores - log_total), 0.0)
    output_gradient = attended_gradient.reshape(
        sequence_list, packed_length, kv_heads, groups, head
    )
    value_heads = value_rows.reshape(sequence_list, packed_length, kv_heads, head)
    value_rows_gradient = jnp.einsum(
        "skglm,slkgd->smkd",
        probs_back.astype(jnp.bfloat16),
        output_gradient,
        preferred_element_type=jnp.float32,
    )
    grad_probs = jnp.einsum(
        "slkgd,smkd->skglm", output_gradient, value_heads, preferred_element_type=jnp.float32
    )
    complete_output = attended_rows.reshape(
        sequence_list, packed_length, kv_heads, groups, head
    ).astype(jnp.float32)
    delta = jnp.transpose(
        jnp.sum(output_gradient.astype(jnp.float32) * complete_output, -1), (0, 2, 3, 1)
    )[..., None]
    grad_scores = (probs_back * (grad_probs - delta)).astype(jnp.bfloat16)
    rotated_query_gradient = jnp.einsum(
        "skglm,smkd->slkgd", grad_scores, every_key_row, preferred_element_type=jnp.float32
    ) * head ** (-0.5)
    rotated_key_gradient = jnp.einsum(
        "skglm,slkgd->smkd", grad_scores, query_rows, preferred_element_type=jnp.float32
    ) * head ** (-0.5)
    token_rows = sequence_list * packed_length
    return (
        rotated_query_gradient.reshape(token_rows, rotated_query_rows.shape[1], head),
        rotated_key_gradient.reshape(token_rows, kv_heads, head),
        value_rows_gradient.reshape(token_rows, kv_heads, head),
    )


def on_device(
    block_input,
    out_grad,
    segments,
    positions,
    attn_gain,
    mlp_gain,
    q_gain,
    k_gain,
    w_q,
    key_matrix,
    value_matrix,
    w_o,
    w_gate,
    w_up,
    w_down,
):
    tokens, width = block_input.shape
    head = q_gain.shape[0]
    heads = w_q.shape[1] // head
    kv_heads = key_matrix.shape[1] // head
    hidden = w_gate.shape[1]
    mask = attention_mask(segments)
    cosine, sine = rope_tables(positions, head // 2)
    inputs = block_input.astype(jnp.float32)
    recip_attn = lax.rsqrt(jnp.mean(inputs * inputs, -1, keepdims=True) + EPSILON)
    normed_rows = (inputs * recip_attn * attn_gain).astype(jnp.bfloat16)
    pieces = (
        lax.all_gather(w_q, "shard", axis=0, tiled=True),
        lax.all_gather(key_matrix, "shard", axis=0, tiled=True),
        lax.all_gather(value_matrix, "shard", axis=0, tiled=True),
    )
    columns = normed_rows
    q_proj, k_proj, v_proj = tuple(
        (
            jnp.dot(columns, weight_piece, preferred_element_type=jnp.float32)
            for weight_piece in pieces
        )
    )
    q_heads = q_proj.reshape(tokens, heads, head)
    key_head_rows = k_proj.reshape(tokens, kv_heads, head)
    q_normed, q_recip = head_norm(q_heads, q_gain)
    k_normed, k_recip = head_norm(key_head_rows, k_gain)
    rotated_query_rows = rotate(q_normed, cosine, sine).astype(jnp.bfloat16)
    rotated_key_rows = rotate(k_normed, cosine, sine).astype(jnp.bfloat16)
    value_rows = v_proj.astype(jnp.bfloat16).reshape(tokens, kv_heads, head)
    attended_rows, log_total = attend_forward(
        rotated_query_rows, rotated_key_rows, value_rows, mask
    )
    attn_out = contract_cols(attended_rows, lax.all_gather(w_o, "shard", axis=0, tiled=True))
    mid = inputs + attn_out
    recip_mlp = lax.rsqrt(jnp.mean(mid * mid, -1, keepdims=True) + EPSILON)
    mlp_in = (mid * recip_mlp * mlp_gain).astype(jnp.bfloat16)
    pieces = (
        lax.all_gather(w_gate, "shard", axis=0, tiled=True),
        lax.all_gather(w_up, "shard", axis=0, tiled=True),
    )
    columns = mlp_in
    gate_pre = jnp.dot(columns, pieces[0], preferred_element_type=jnp.float32)
    up_pre = jnp.dot(columns, pieces[1], preferred_element_type=jnp.float32)
    sigma = jax.nn.sigmoid(gate_pre)
    silu_gate = gate_pre * sigma
    act = (silu_gate * up_pre).astype(jnp.bfloat16)
    mlp_out = contract_cols(act, lax.all_gather(w_down, "shard", axis=0, tiled=True))
    output = (mid + mlp_out).astype(jnp.bfloat16)
    grad_top = out_grad.astype(jnp.float32)
    columns = out_grad
    grad_act = jnp.dot(
        columns,
        lax.all_gather(w_down, "shard", axis=0, tiled=True),
        preferred_element_type=jnp.float32,
    )
    grad_gate = (grad_act * up_pre * sigma * (1.0 + gate_pre * (1.0 - sigma))).astype(jnp.bfloat16)
    grad_up = (grad_act * silu_gate).astype(jnp.bfloat16)
    pieces = (
        lax.all_gather(w_gate, "shard", axis=0, tiled=True),
        lax.all_gather(w_up, "shard", axis=0, tiled=True),
    )
    part = contract_cols(grad_gate, pieces[0]) + contract_cols(grad_up, pieces[1])
    grad_mlp_in = part
    mlp_right = jnp.concatenate([grad_gate, grad_up], 1)
    left_in = mlp_in
    left_grad = out_grad
    mlp_grads = lax.psum_scatter(
        jnp.concatenate([contract_rows(left_in, mlp_right), contract_rows(left_grad, act)], 1),
        "shard",
        scatter_dimension=0,
        tiled=True,
    )
    grad_mid_part, mlp_gain_part = norm_back(grad_mlp_in, mid, recip_mlp, mlp_gain, 0)
    grad_mid = grad_top + grad_mid_part
    grad_mid_b = grad_mid.astype(jnp.bfloat16)
    columns = grad_mid_b
    attended_gradient = jnp.dot(
        columns,
        lax.all_gather(w_o, "shard", axis=0, tiled=True),
        preferred_element_type=jnp.float32,
    ).astype(jnp.bfloat16)
    rotated_query_gradient, rotated_key_gradient, value_rows_gradient = attend_backward(
        rotated_query_rows,
        rotated_key_rows,
        value_rows,
        attended_rows,
        attended_gradient,
        log_total,
        mask,
    )
    grad_qh, q_gain_part = norm_back(
        unrotate(rotated_query_gradient, cosine, sine), q_heads, q_recip, q_gain, (0, 1)
    )
    key_heads_gradient, k_gain_part = norm_back(
        unrotate(rotated_key_gradient, cosine, sine), key_head_rows, k_recip, k_gain, (0, 1)
    )
    grad_q = grad_qh.reshape(tokens, heads * head).astype(jnp.bfloat16)
    key_gradient = key_heads_gradient.reshape(tokens, kv_heads * head).astype(jnp.bfloat16)
    value_gradient = value_rows_gradient.reshape(tokens, kv_heads * head).astype(jnp.bfloat16)
    pieces = (
        lax.all_gather(w_q, "shard", axis=0, tiled=True),
        lax.all_gather(key_matrix, "shard", axis=0, tiled=True),
        lax.all_gather(value_matrix, "shard", axis=0, tiled=True),
    )
    part = (
        contract_cols(grad_q, pieces[0])
        + contract_cols(key_gradient, pieces[1])
        + contract_cols(value_gradient, pieces[2])
    )
    attn_right = jnp.concatenate([grad_q, key_gradient, value_gradient], 1)
    left_in = normed_rows
    left_grad = grad_mid_b
    attn_grads = lax.psum_scatter(
        jnp.concatenate(
            [contract_rows(left_in, attn_right), contract_rows(left_grad, attended_rows)], 1
        ),
        "shard",
        scatter_dimension=0,
        tiled=True,
    )
    grad_in_part, attn_gain_part = norm_back(part, inputs, recip_attn, attn_gain, 0)
    grad_input = grad_mid + grad_in_part
    gain_totals = lax.psum(
        (attn_gain_part, mlp_gain_part, q_gain_part, k_gain_part), ("rep", "shard")
    )
    attn_total, mlp_total = (
        lax.psum(attn_grads.astype(jnp.bfloat16), "rep").astype(jnp.float32),
        lax.psum(mlp_grads.astype(jnp.bfloat16), "rep").astype(jnp.float32),
    )
    q_cols = heads * head
    k_cols = kv_heads * head
    grad_w_q = attn_total[:, :q_cols]
    grad_w_k = attn_total[:, q_cols : q_cols + k_cols]
    grad_w_v = attn_total[:, q_cols + k_cols : q_cols + 2 * k_cols]
    grad_w_o = attn_total[:, q_cols + 2 * k_cols :]
    grad_w_gate = mlp_total[:, :hidden]
    grad_w_up = mlp_total[:, hidden : 2 * hidden]
    grad_w_down = mlp_total[:, 2 * hidden :]
    return (
        output,
        grad_input,
        grad_w_q,
        grad_w_k,
        grad_w_v,
        grad_w_o,
        grad_w_gate,
        grad_w_up,
        grad_w_down,
        gain_totals[0],
        gain_totals[1],
        gain_totals[2],
        gain_totals[3],
    )


def solution(mesh):
    placed = (
        P(("rep", "shard"), None),
        P(("rep", "shard"), None),
        P(("rep", "shard"), None),
        P(("rep", "shard"), None),
        P(),
        P(),
        P(),
        P(),
        P("shard", None),
        P("shard", None),
        P("shard", None),
        P("shard", None),
        P("shard", None),
        P("shard", None),
        P("shard", None),
    )
    return jax.shard_map(
        on_device,
        mesh=mesh,
        in_specs=placed,
        out_specs=(
            P(("rep", "shard"), None),
            P(("rep", "shard"), None),
            P("shard", None),
            P("shard", None),
            P("shard", None),
            P("shard", None),
            P("shard", None),
            P("shard", None),
            P("shard", None),
            P(),
            P(),
            P(),
            P(),
        ),
        check_vma=False,
    )
```

profile of v0, /device:TPU:0, one launch (start us, length us, event | category | flops | bytes accessed | tf_op | source)
XLA Modules:
  0.0 2806.3 jit_solution(15419628978582923309)
XLA Ops:
  14.5 49.1 %all-gather.8.cloned.1.call-done = bf16[2048,1024]{1,0:T(8,128)(2,1)} async-done(((bf16[128,1024]{1,0:T(8,128)(2,1)}), bf16[2048,1024]{1,0:T(8,128)(2,1)}) %all-gather.8.cloned.1.call-update) | async-done | bytes 4194320 | tf_op jit(solution)/shard_map/all_gather | solution.py:177
  63.5 2.9 fusion.19
  66.6 48.2 %all-gather.10.cloned.1.call-done = bf16[2048,1024]{1,0:T(8,128)(2,1)} async-done(((bf16[128,1024]{1,0:T(8,128)(2,1)}), bf16[2048,1024]{1,0:T(8,128)(2,1)}) %all-gather.10.cloned.1.call-update) | async-done | bytes 4194320 | tf_op jit(solution)/shard_map/all_gather | solution.py:176
  114.8 2.9 fusion.66
  119.3 71.0 %all-gather.12.cloned.1.call-done = bf16[2048,2048]{1,0:T(8,128)(2,1)} async-done(((bf16[128,2048]{1,0:T(8,128)(2,1)}), bf16[2048,2048]{1,0:T(8,128)(2,1)}) %all-gather.12.cloned.1.call-update) | async-done | bytes 8388624 | tf_op jit(solution)/shard_map/all_gather | solution.py:175
  190.4 4.7 fusion.64
  200.2 65.4 %all-gather.14.cloned.1.call-done = bf16[2048,2048]{1,0:T(8,128)(2,1)} async-done(((bf16[128,2048]{1,0:T(8,128)(2,1)}), bf16[2048,2048]{1,0:T(8,128)(2,1)}) %all-gather.14.cloned.1.call-update) | async-done | bytes 8388624 | tf_op jit(solution)/shard_map/all_gather | solution.py:196
  265.6 6.4 multiply_reduce_fusion.4
  272.8 121.1 %all-gather.18.cloned.1.call-done = bf16[2048,6144]{1,0:T(8,128)(2,1)} async-done(((bf16[128,6144]{1,0:T(8,128)(2,1)}), bf16[2048,6144]{1,0:T(8,128)(2,1)}) %all-gather.18.cloned.1.call-update) | async-done | bytes 25165840 | tf_op jit(solution)/shard_map/all_gather | solution.py:202
  393.9 13.7 fusion.75
  407.6 116.4 %all-gather.16.cloned.1.call-done = bf16[2048,6144]{1,0:T(8,128)(2,1)} async-done(((bf16[128,6144]{1,0:T(8,128)(2,1)}), bf16[2048,6144]{1,0:T(8,128)(2,1)}) %all-gather.16.cloned.1.call-update) | async-done | bytes 25165840 | tf_op jit(solution)/shard_map/all_gather | solution.py:201
  524.0 13.2 fusion.74
  537.2 117.0 %all-gather.20.cloned.1.call-done = bf16[2048,6144]{1,0:T(8,128)(2,1)} async-done(((bf16[128,6144]{1,0:T(8,128)(2,1)}), bf16[2048,6144]{1,0:T(8,128)(2,1)}) %all-gather.20.cloned.1.call-update) | async-done | bytes 25165840 | tf_op jit(solution)/shard_map/all_gather | solution.py:210
  654.2 14.8 multiply_convert_fusion
  668.9 13.5 fusion.76
  682.5 15.2 multiply_reduce_fusion
  698.3 1.7 multiply_add_fusion.1
  700.0 5.8 convolution_convert_fusion
  705.8 2.1 copy.172
  708.0 2.2 copy.132
  710.2 1.6 multiply_reduce_fusion.2
  711.8 2.1 fusion.18
  715.9 1.5 convolution_multiply_fusion
  717.4 8.1 fusion.50
  725.7 2.1 fusion.72
  730.5 2.4 copy.169
  732.9 1.5 multiply_add_fusion
  734.5 1.7 multiply_reduce_fusion.1
  738.3 2.2 fusion.30
  740.5 13.6 fusion.31
  754.1 33.6 %pad_maximum_fusion.1 = f32[2048,6144]{1,0:T(8,128)} fusion(f32[2048,2048]{1,0:T(8,128)} %fusion.50, f32[2048,4096]{1,0:T(8,128)} %fusion.31), kind=kLoop, calls=%fused_computation.1 | loop fusion | flops 12582912 | bytes 100663296 | tf_op jit(solution)/shard_map/concatenate | solution.py:277
  789.1 32.8 %convolution_bitcast_fusion = f32[2048,6144]{1,0:T(8,128)} fusion(bf16[128,6144]{1,0:T(8,128)(2,1)S(1)} %copy-done.13, bf16[128,2048]{1,0:T(8,128)(2,1)} %param.16), kind=kOutput, calls=%fused_computation.2 | convolution fusion | flops 3221225472 | bytes 52428800 | tf_op jit(solution)/shard_map/dot_general | solution.py:52
  822.0 48.1 %fusion = f32[2048,12288]{1,0:T(8,128)} fusion(bf16[128,2048]{1,0:T(8,128)(2,1)} %copy-done.15, bf16[128,6144]{1,0:T(8,128)(2,1)} %get-tuple-element.25, bf16[128,6144]{1,0:T(8,128)(2,1)S(1)} %copy-done.14), kind=kOutput, calls=%fused_computation.3 | convolution fusion | flops 6448742400 | bytes 104333312 | tf_op jit(solution)/shard_map/dot_general | solution.py:52
  870.1 100.2 %pad_maximum_fusion = f32[2048,18432]{1,0:T(8,128)} fusion(f32[2048,6144]{1,0:T(8,128)} %convolution_bitcast_fusion, f32[2048,12288]{1,0:T(8,128)} %fusion), kind=kLoop, calls=%fused_computation | loop fusion | flops 37748736 | bytes 301989888 | tf_op jit(solution)/shard_map/concatenate | solution.py:231
  970.6 285.1 %reduce-scatter.3.cloned.1.call-done = f32[128,6144]{1,0:T(8,128)} async-done(((f32[2048,6144]{1,0:T(8,128)}), f32[128,6144]{1,0:T(8,128)}) %reduce-scatter.3.cloned.1.call-update) | async-done | bytes 3145744 | tf_op jit(solution)/shard_map/reduce_scatter | solution.py:276
  1255.7 3.2 convert_element_type.156
  1258.9 1370.2 %reduce-scatter.5.cloned.1.call-done = f32[128,18432]{1,0:T(8,128)} async-done(((f32[2048,18432]{1,0:T(8,128)}), f32[128,18432]{1,0:T(8,128)}) %reduce-scatter.5.cloned.1.call-update) | async-done | bytes 9437200 | tf_op jit(solution)/shard_map/reduce_scatter | solution.py:230
  2629.1 6.5 convert_element_type.158
  2636.7 6.4 fusion.77
  2643.2 1.5 convolution_add_fusion.1
  2645.6 2.7 fusion.25
  2648.2 40.2 %all-reduce = (f32[2048]{0:T(1024)}, f32[2048]{0:T(1024)}, f32[128]{0:T(128)}, f32[128]{0:T(128)}) all-reduce(f32[2048]{0:T(1024)S(1)} %get-tuple-element.15, f32[2048]{0:T(1024)S(1)} %copy-done.50, f32[128]{0:T(128)S(1)} %bitcast_reduce_fusion, f32[128]{0:T(128)S(1)} %bitcast_reduce_fusion.1), channel_id=1, replica_groups=mesh['rep'=2,'shard'=16] {'rep','shard'}, use_global_device_ids=true, to_apply=%region_16.17 | all-reduce | flops 4352 | bytes 34816 | tf_op jit(solution)/shard_map/psum | solution.py:286
  2688.5 2.6 fusion.24
  2691.0 14.2 fusion.5
  2705.2 84.7 %all-reduce.4.cloned.1.call-done = (bf16[128,6144]{1,0:T(8,128)(2,1)}, bf16[128,18432]{1,0:T(8,128)(2,1)}) async-done(((bf16[128,6144]{1,0:T(8,128)(2,1)}, bf16[128,18432]{1,0:T(8,128)(2,1)}), (bf16[128,6144]{1,0:T(8,128)(2,1)}, bf16[128,18432]{1,0:T(8,128)(2,1)})) %all-reduce.4.cloned.1.call-update) | async-done | bytes 6291472 | tf_op jit(solution)/shard_map/psum | solution.py:290
  2790.0 2.3 fusion.71
  2792.2 2.8 fusion.70
  2795.0 4.0 fusion.69
  (187 shorter events, 25.6 us)
Async XLA Ops:
  7.2 4.8 copy-start
  7.2 5.0 copy-start.59
  7.2 5.0 copy-start.55
  7.2 5.6 copy-start.57
  7.2 6.2 copy-start.58
  7.2 56.3 %copy-start.37 = (f32[2048]{0:T(1024)S(1)}, f32[2048]{0:T(1024)}, u32[]{:S(2)}) copy-start(f32[2048]{0:T(1024)} %param.19) | copy-start | bytes 24580
  7.2 56.3 %all-gather.8.cloned.1.call-start = ((), (), s32[]{:S(2)}) async-start(), calls=%async_computation.2 | async-start | bytes 4456448 | tf_op jit(solution)/shard_map/all_gather | solution.py:177
  8.0 106.8 %all-gather.10.cloned.1.call-start = ((), (), s32[]{:S(2)}) async-start(), calls=%async_computation.3 | async-start | bytes 4456448 | tf_op jit(solution)/shard_map/all_gather | solution.py:176
  8.7 181.6 %all-gather.12.cloned.1.call-start = ((), (), s32[]{:S(2)}) async-start(), calls=%async_computation.4 | async-start | bytes 8912896 | tf_op jit(solution)/shard_map/all_gather | solution.py:175
  9.5 256.1 %all-gather.14.cloned.1.call-start = ((), (), s32[]{:S(2)}) async-start(), calls=%async_computation.5 | async-start | bytes 8912896 | tf_op jit(solution)/shard_map/all_gather | solution.py:196
  10.0 383.8 %all-gather.18.cloned.1.call-start = ((), (), s32[]{:S(2)}) async-start(), calls=%async_computation.7 | async-start | bytes 26738688 | tf_op jit(solution)/shard_map/all_gather | solution.py:202
  10.6 513.3 %all-gather.16.cloned.1.call-start = ((), (), s32[]{:S(2)}) async-start(), calls=%async_computation.6 | async-start | bytes 26738688 | tf_op jit(solution)/shard_map/all_gather | solution.py:201
  11.2 643.0 %all-gather.20.cloned.1.call-start = ((), (), s32[]{:S(2)}) async-start(), calls=%async_computation.8 | async-start | bytes 26738688 | tf_op jit(solution)/shard_map/all_gather | solution.py:210
  12.0 1243.7 %reduce-scatter.3.cloned.1.call-start = ((), (), s32[]{:S(2)}) async-start(), calls=%async_computation.9 | async-start | bytes 53477376 | tf_op jit(solution)/shard_map/reduce_scatter | solution.py:276
  12.2 178.1 %copy-start.46 = (f32[128]{0:T(128)}, f32[128]{0:T(128)S(1)}, u32[]{:S(2)}) copy-start(f32[128]{0:T(128)S(1)} %add_rsqrt_fusion.3) | copy-start | bytes 1540
  66.5 132.4 %copy-start.36 = (bf16[16,8,8,128]{3,2,1,0:T(8,128)(2,1)}, bf16[16,8,8,128]{3,2,1,0:T(8,128)(2,1)S(1)}, u32[]{:S(2)}) copy-start(bf16[16,8,8,128]{3,2,1,0:T(8,128)(2,1)S(1)} %copy.175) | copy-start | bytes 786436
  119.3 78.8 %copy-start.28 = (bf16[128,8,64]{2,0,1:T(8,128)(2,1)}, bf16[128,8,64]{2,0,1:T(8,128)(2,1)S(1)}, u32[]{:S(2)}) copy-start(bf16[128,8,64]{2,0,1:T(8,128)(2,1)S(1)} %get-tuple-element.50) | copy-start | bytes 393220
  198.2 67.4 %copy-start.22 = (bf16[128,16,64]{2,0,1:T(8,128)(2,1)}, bf16[128,16,64]{2,0,1:T(8,128)(2,1)S(1)}, u32[]{:S(2)}) copy-start(bf16[128,16,64]{2,0,1:T(8,128)(2,1)S(1)} %copy.127) | copy-start | bytes 786436
  200.1 71.8 %copy-start.24 = (bf16[8,128,2,128]{3,1,2,0:T(8,128)(2,1)}, bf16[8,128,2,128]{3,1,2,0:T(8,128)(2,1)S(1)}, u32[]{:S(2)}) copy-start(bf16[8,128,2,128]{3,1,2,0:T(8,128)(2,1)S(1)} %convolution_convert_fusion.1) | copy-start | bytes 1572868
  265.6 7.1 copy-start.42
  271.9 426.4 %copy-start.2 = (f32[128,2048]{1,0:T(8,128)}, f32[128,2048]{1,0:T(8,128)S(1)}, u32[]{:S(2)}) copy-start(f32[128,2048]{1,0:T(8,128)S(1)} %get-tuple-element.56) | copy-start | bytes 3145732
  272.0 121.9 %copy-start.54 = (f32[128]{0:T(128)}, f32[128]{0:T(128)S(1)}, u32[]{:S(2)}) copy-start(f32[128]{0:T(128)S(1)} %add_rsqrt_fusion.2) | copy-start | bytes 1540
  272.8 251.1 %copy-start.15 = (bf16[128,2048]{1,0:T(8,128)(2,1)}, bf16[128,2048]{1,0:T(8,128)(2,1)S(1)}, u32[]{:S(2)}) copy-start(bf16[128,2048]{1,0:T(8,128)(2,1)S(1)} %multiply_convert_fusion.3) | copy-start | bytes 1572868
  407.6 246.6 %copy-start.32 = (bf16[128,2048]{1,0:T(8,128)(2,1)S(1)}, bf16[128,2048]{1,0:T(8,128)(2,1)}, u32[]{:S(2)}) copy-start(bf16[128,2048]{1,0:T(8,128)(2,1)} %param.16) | copy-start | bytes 1572868
  700.0 17.4 copy-start.4
  705.8 5.9 copy-start.10
  705.8 6.0 copy-start.43
  710.2 5.2 copy-start.21
  710.2 5.2 copy-start.23
  710.2 5.7 copy-start.29
  711.8 5.6 copy-start.25
  717.4 8.1 copy-start.30
  728.6 5.9 copy-start.8
  732.9 3.8 copy-start.33
  732.9 3.8 copy-start.52
  734.5 3.8 copy-start.17
  734.5 3.8 copy-start.49
  736.7 3.8 copy-start.47
  737.6 16.4 copy-start.26
  740.5 13.6 copy-start.18
  787.7 1841.4 %reduce-scatter.5.cloned.1.call-start = ((), (), s32[]{:S(2)}) async-start(), calls=%async_computation.10 | async-start | bytes 160432128 | tf_op jit(solution)/shard_map/reduce_scatter | solution.py:230
  789.1 32.8 %copy-start.14 = (bf16[128,6144]{1,0:T(8,128)(2,1)S(1)}, bf16[128,6144]{1,0:T(8,128)(2,1)}, u32[]{:S(2)}) copy-start(bf16[128,6144]{1,0:T(8,128)(2,1)} %get-tuple-element.26) | copy-start | bytes 4718596
  970.3 1819.6 %all-reduce.4.cloned.1.call-start = ((), (), s32[]{:S(2)}) async-start(), calls=%async_computation.11 | async-start | bytes 12582912 | tf_op jit(solution)/shard_map/psum | solution.py:290
  2636.7 6.4 copy-start.12
  2636.7 6.4 copy-start.27
  2645.5 42.9 %copy-start.5 = (f32[128,2048]{1,0:T(8,128)S(1)}, f32[128,2048]{1,0:T(8,128)}, u32[]{:S(2)}) copy-start(f32[128,2048]{1,0:T(8,128)} %copy-done.4) | copy-start | bytes 3145732
  2645.5 45.5 %copy-start.3 = (f32[128,2048]{1,0:T(8,128)S(1)}, f32[128,2048]{1,0:T(8,128)}, u32[]{:S(2)}) copy-start(f32[128,2048]{1,0:T(8,128)} %copy-done.2) | copy-start | bytes 3145732
  2790.0 5.0 copy-start.6
  (22 other events, 41.8 us)
Sparse Core Ops, SparseCore 0:
  10.2 53.2 all-gather.7
  65.7 49.0 all-gather.9
  116.9 73.3 all-gather.11
  192.4 73.1 all-gather.13
  267.0 126.8 all-gather.17
  395.3 128.5 all-gather.15
  525.5 128.5 all-gather.19
  787.9 467.7 reduce-scatter.2
  1259.9 1369.1 reduce-scatter.4
  2635.8 154.1 all-reduce.3
where the time goes:
time: 2820 us; the launch traced here: 2810 us
  waiting for transfers between devices  2330 us (83%)
  matrix products  227 us (8%)
  other arithmetic  162 us (6%)
  blocking collectives  40.2 us (1%)
  local copies, waits for them, and re-layouts  28.5 us (1%)
    reduce_scatter x1, waiting for transfers between devices, on_device(): lax.psum_scatter(jnp.concatenate([contract_rows(left_in, mlp_right), cont...  1370 us
    reduce_scatter x1, waiting for transfers between devices, on_device(): lax.psum_scatter(jnp.concatenate([contract_rows(left_in, attn_right), con...  285 us
    all_gather x1, waiting for transfers between devices, on_device(): lax.all_gather(w_up, 'shard', axis=0, tiled=True)  121 us
    all_gather x1, waiting for transfers between devices, on_device(): lax.all_gather(w_down, 'shard', axis=0, tiled=True)  117 us
    all_gather x1, waiting for transfers between devices, on_device(): lax.all_gather(w_gate, 'shard', axis=0, tiled=True)  116 us
    dot_general x4, matrix products, contract_rows(): lax.dot_general(left, right, (((0,), (0,)), ((), ())), preferred_element_...  103 us
    concatenate x1, other arithmetic, on_device(): jnp.concatenate([contract_rows(left_in, mlp_right), contract_rows(left_gr...  100 us
    psum x1, waiting for transfers between devices, on_device(): lax.psum(attn_grads.astype(jnp.bfloat16), 'rep').astype(jnp.float32)  84.7 us
  transfers between devices with their start and end apart: 10, of which 10 were waited for; matrix products, arithmetic and copies ran while one was open for 9% of the time, Pallas kernels for 0%

commit v1 on v0

--- a/solution.py
+++ b/solution.py
@@ -7,6 +7,24 @@
 EPSILON = 1e-06
 ROPE_BASE = 1000000.0
 NEG_FILL = -1e30
+
+
+def ring_gather(value, axis, dim):
+    ways, here, hop = (lax.axis_size(axis), lax.axis_index(axis), value.shape[dim])
+    dims = [n * ways if d == dim else n for d, n in enumerate(value.shape)]
+    full = lax.dynamic_update_slice_in_dim(
+        jnp.zeros(dims, value.dtype), value, here * hop, axis=dim
+    )
+    going_up = going_down = value
+    for far in range(1, ways // 2 + 1):
+        going_up = lax.ppermute(going_up, axis, [(d, (d + 1) % ways) for d in range(ways)])
+        full = lax.dynamic_update_slice_in_dim(full, going_up, (here - far) % ways * hop, axis=dim)
+        if 2 * far < ways:
+            going_down = lax.ppermute(going_down, axis, [(d, (d - 1) % ways) for d in range(ways)])
+            full = lax.dynamic_update_slice_in_dim(
+                full, going_down, (here + far) % ways * hop, axis=dim
+            )
+    return full
 
 
 def rope_tables(positions, half):
@@ -197,10 +215,7 @@
     mid = inputs + attn_out
     recip_mlp = lax.rsqrt(jnp.mean(mid * mid, -1, keepdims=True) + EPSILON)
     mlp_in = (mid * recip_mlp * mlp_gain).astype(jnp.bfloat16)
-    pieces = (
-        lax.all_gather(w_gate, "shard", axis=0, tiled=True),
-        lax.all_gather(w_up, "shard", axis=0, tiled=True),
-    )
+    pieces = (lax.all_gather(w_gate, "shard", axis=0, tiled=True), ring_gather(w_up, "shard", 0))
     columns = mlp_in
     gate_pre = jnp.dot(columns, pieces[0], preferred_element_type=jnp.float32)
     up_pre = jnp.dot(columns, pieces[1], preferred_element_type=jnp.float32)

time: 2820 us -> 2910 us (1.032)
  starting transfers between devices: 0.64 us -> 133 us
  waiting for transfers between devices: 2330 us -> 2270 us
  local copies, waits for them, and re-layouts: 28.5 us -> 65.8 us
    ppermute x0 -> x15, waiting for transfers between devices: none -> 158 us  [the longest x8 158 us: ring_gather(): lax.ppermute(going_up, axis, [(d, (d + 1) % ways) for d in range(ways)])]
    ppermute x0 -> x15, starting transfers between devices: none -> 133 us  [the longest x8 128 us: ring_gather(): lax.ppermute(going_up, axis, [(d, (d + 1) % ways) for d in range(ways)])]
    all_gather x1, waiting for transfers between devices: 71 us -> 0.01 us  [on_device(): lax.all_gather(w_q, 'shard', axis=0, tiled=True)]
    all_gather x1, waiting for transfers between devices: 49.1 us -> 0.01 us  [on_device(): lax.all_gather(value_matrix, 'shard', axis=0, tiled=True)]
    all_gather x1, waiting for transfers between devices: 48.2 us -> 0.01 us  [on_device(): lax.all_gather(key_matrix, 'shard', axis=0, tiled=True)]
    all_gather x1, waiting for transfers between devices: 65.4 us -> 31.2 us  [on_device(): lax.all_gather(w_o, 'shard', axis=0, tiled=True)]
    dynamic_update_slice x0 -> x16, local copies, waits for them, and re-layouts: none -> 29.1 us  [the longest x8 16 us: ring_gather(): lax.dynamic_update_slice_in_dim(full, going_up, (here - far) % ways * hop...]
  transfers between devices with their start and end apart: 10 -> 25, of which waited for: 10 -> 15; matrix products, arithmetic and copies ran while one was open for 9% -> 11% of each run, Pallas kernels for 0% -> 0%
where the time goes in v1:
time: 2910 us
  waiting for transfers between devices  2270 us (78%)
  matrix products  223 us (8%)
  other arithmetic  162 us (6%)
  starting transfers between devices  133 us (5%)
  local copies, waits for them, and re-layouts  65.8 us (2%)
  blocking collectives  40.2 us (1%)
    reduce_scatter x1, waiting for transfers between devices, on_device(): lax.psum_scatter(jnp.concatenate([contract_rows(left_in, mlp_right), cont...  1370 us
    reduce_scatter x1, waiting for transfers between devices, on_device(): lax.psum_scatter(jnp.concatenate([contract_rows(left_in, attn_right), con...  285 us
    ppermute x8, waiting for transfers between devices, ring_gather(): lax.ppermute(going_up, axis, [(d, (d + 1) % ways) for d in range(ways)])  158 us
    ppermute x8, starting transfers between devices, ring_gather(): lax.ppermute(going_up, axis, [(d, (d + 1) % ways) for d in range(ways)])  128 us
    all_gather x1, waiting for transfers between devices, on_device(): lax.all_gather(w_gate, 'shard', axis=0, tiled=True)  123 us
    all_gather x1, waiting for transfers between devices, on_device(): lax.all_gather(w_down, 'shard', axis=0, tiled=True)  117 us
    dot_general x4, matrix products, contract_rows(): lax.dot_general(left, right, (((0,), (0,)), ((), ())), preferred_element_...  103 us
    concatenate x1, other arithmetic, on_device(): jnp.concatenate([contract_rows(left_in, mlp_right), contract_rows(left_gr...  100 us
  transfers between devices with their start and end apart: 25, of which 15 were waited for; matrix products, arithmetic and copies ran while one was open for 11% of the time, Pallas kernels for 0%

profile of v1, /device:TPU:0, one launch (start us, length us, event | category | flops | bytes accessed | tf_op | source)
XLA Modules:
  0.0 2905.5 jit_solution(8663295006173832211)
XLA Ops:
  12.5 5.1 collective-permute-start.1
  18.4 24.6 collective-permute-done
  43.0 13.6 collective-permute-start.2
  58.2 8.7 broadcast_in_dim.26
  68.1 7.7 collective-permute-done.2
  75.8 21.4 collective-permute-start.4
  97.2 2.8 constant_dynamic-update-slice_fusion.14
  104.0 14.8 collective-permute-done.4
  118.8 26.7 collective-permute-start.6
  149.2 17.3 collective-permute-done.6
  166.5 15.2 collective-permute-start.8
  185.8 2.9 fusion.19
  189.5 14.3 collective-permute-done.8
  203.7 21.4 collective-permute-start.10
  225.1 2.9 fusion.66
  232.1 29.3 %collective-permute-done.10 = bf16[128,6144]{1,0:T(8,128)(2,1)} collective-permute-done((bf16[128,6144]{1,0:T(8,128)(2,1)}, bf16[128,6144]{1,0:T(8,128)(2,1)}, u32[]{:S(2)}, u32[]{:S(2)}) %collective-permute-start.10) | collective-permute-done | bytes 1572896 | tf_op jit(solution)/shard_map/ppermute | solution.py:20
  261.5 18.2 collective-permute-start.12
  279.9 2.8 constant_dynamic-update-slice_fusion.5
  285.5 20.7 collective-permute-done.12
  306.3 10.6 collective-permute-start.14
  320.6 29.2 %collective-permute-done.14 = bf16[128,6144]{1,0:T(8,128)(2,1)S(1)} collective-permute-done((bf16[128,6144]{1,0:T(8,128)(2,1)S(1)}, bf16[128,6144]{1,0:T(8,128)(2,1)S(1)}, u32[]{:S(2)}, u32[]{:S(2)}) %collective-permute-start.14) | collective-permute-done | bytes 1572896 | tf_op jit(solution)/shard_map/ppermute | solution.py:20
  351.1 5.2 fusion.64
  361.4 31.2 %all-gather.14.cloned.1.call-done = bf16[2048,2048]{1,0:T(8,128)(2,1)} async-done(((bf16[128,2048]{1,0:T(8,128)(2,1)}), bf16[2048,2048]{1,0:T(8,128)(2,1)}) %all-gather.14.cloned.1.call-update) | async-done | bytes 8388624 | tf_op jit(solution)/shard_map/all_gather | solution.py:214
  392.6 6.4 multiply_reduce_fusion.4
  399.9 122.8 %all-gather.16.cloned.1.call-done = bf16[2048,6144]{1,0:T(8,128)(2,1)} async-done(((bf16[128,6144]{1,0:T(8,128)(2,1)}), bf16[2048,6144]{1,0:T(8,128)(2,1)}) %all-gather.16.cloned.1.call-update) | async-done | bytes 25165840 | tf_op jit(solution)/shard_map/all_gather | solution.py:218
  522.7 13.3 fusion.74
  536.0 116.8 %all-gather.18.cloned.1.call-done = bf16[2048,6144]{1,0:T(8,128)(2,1)} async-done(((bf16[128,6144]{1,0:T(8,128)(2,1)}), bf16[2048,6144]{1,0:T(8,128)(2,1)}) %all-gather.18.cloned.1.call-update) | async-done | bytes 25165840 | tf_op jit(solution)/shard_map/all_gather | solution.py:225
  652.7 11.0 fusion.75
  663.8 13.0 multiply_convert_fusion
  676.8 13.8 fusion.76
  690.6 92.3 %all-gather.20.cloned.1.call-done = bf16[2048,6144]{1,0:T(8,128)(2,1)} async-done(((bf16[128,6144]{1,0:T(8,128)(2,1)}), bf16[2048,6144]{1,0:T(8,128)(2,1)}) %all-gather.20.cloned.1.call-update) | async-done | bytes 25165840 | tf_op jit(solution)/shard_map/all_gather | solution.py:238
  782.9 15.2 multiply_reduce_fusion
  800.5 5.8 convolution_convert_fusion
  817.7 8.2 fusion.50
  839.7 13.6 fusion.31
  853.3 33.6 %pad_maximum_fusion.1 = f32[2048,6144]{1,0:T(8,128)} fusion(f32[2048,2048]{1,0:T(8,128)} %fusion.50, f32[2048,4096]{1,0:T(8,128)} %fusion.31), kind=kLoop, calls=%fused_computation.1 | loop fusion | flops 12582912 | bytes 100663296 | tf_op jit(solution)/shard_map/concatenate | solution.py:292
  888.3 32.9 %convolution_bitcast_fusion = f32[2048,6144]{1,0:T(8,128)} fusion(bf16[128,6144]{1,0:T(8,128)(2,1)S(1)} %copy-done.13, bf16[128,2048]{1,0:T(8,128)(2,1)} %param.16), kind=kOutput, calls=%fused_computation.2 | convolution fusion | flops 3221225472 | bytes 52428800 | tf_op jit(solution)/shard_map/dot_general | solution.py:70
  921.2 48.1 %fusion = f32[2048,12288]{1,0:T(8,128)} fusion(bf16[128,2048]{1,0:T(8,128)(2,1)} %copy-done.18, bf16[128,6144]{1,0:T(8,128)(2,1)} %get-tuple-element.25, bf16[128,6144]{1,0:T(8,128)(2,1)S(1)} %copy-done.14), kind=kOutput, calls=%fused_computation.3 | convolution fusion | flops 6448742400 | bytes 104333312 | tf_op jit(solution)/shard_map/dot_general | solution.py:70
  969.3 100.3 %pad_maximum_fusion = f32[2048,18432]{1,0:T(8,128)} fusion(f32[2048,6144]{1,0:T(8,128)} %convolution_bitcast_fusion, f32[2048,12288]{1,0:T(8,128)} %fusion), kind=kLoop, calls=%fused_computation | loop fusion | flops 37748736 | bytes 301989888 | tf_op jit(solution)/shard_map/concatenate | solution.py:246
  1069.9 285.0 %reduce-scatter.3.cloned.1.call-done = f32[128,6144]{1,0:T(8,128)} async-done(((f32[2048,6144]{1,0:T(8,128)}), f32[128,6144]{1,0:T(8,128)}) %reduce-scatter.3.cloned.1.call-update) | async-done | bytes 3145744 | tf_op jit(solution)/shard_map/reduce_scatter | solution.py:291
  1354.9 3.2 convert_element_type.156
  1358.1 1370.2 %reduce-scatter.5.cloned.1.call-done = f32[128,18432]{1,0:T(8,128)} async-done(((f32[2048,18432]{1,0:T(8,128)}), f32[128,18432]{1,0:T(8,128)}) %reduce-scatter.5.cloned.1.call-update) | async-done | bytes 9437200 | tf_op jit(solution)/shard_map/reduce_scatter | solution.py:245
  2728.3 6.5 convert_element_type.158
  2735.8 6.4 fusion.77
  2747.3 40.2 %all-reduce = (f32[2048]{0:T(1024)}, f32[2048]{0:T(1024)}, f32[128]{0:T(128)}, f32[128]{0:T(128)}) all-reduce(f32[2048]{0:T(1024)S(1)} %get-tuple-element.15, f32[2048]{0:T(1024)S(1)} %copy-done.53, f32[128]{0:T(128)S(1)} %bitcast_reduce_fusion, f32[128]{0:T(128)S(1)} %bitcast_reduce_fusion.1), channel_id=1, replica_groups=mesh['rep'=2,'shard'=16] {'rep','shard'}, use_global_device_ids=true, to_apply=%region_16.17 | all-reduce | flops 4352 | bytes 34816 | tf_op jit(solution)/shard_map/psum | solution.py:301
  2790.2 14.2 fusion.5
  2804.4 84.8 %all-reduce.4.cloned.1.call-done = (bf16[128,6144]{1,0:T(8,128)(2,1)}, bf16[128,18432]{1,0:T(8,128)(2,1)}) async-done(((bf16[128,6144]{1,0:T(8,128)(2,1)}, bf16[128,18432]{1,0:T(8,128)(2,1)}), (bf16[128,6144]{1,0:T(8,128)(2,1)}, bf16[128,18432]{1,0:T(8,128)(2,1)})) %all-reduce.4.cloned.1.call-update) | async-done | bytes 6291472 | tf_op jit(solution)/shard_map/psum | solution.py:305
  2894.2 4.0 fusion.69
  (240 shorter events, 81.9 us)
Async XLA Ops:
  7.2 10.6 copy-start.62
  7.2 10.6 copy-start.58
  7.2 49.3 %copy-start.60 = (f32[128]{0:T(128)S(1)}, f32[128]{0:T(128)}, u32[]{:S(2)}) copy-start(f32[128]{0:T(128)} %param.21) | copy-start | bytes 1540
  7.2 50.0 %copy-start.61 = (s32[1,128]{1,0:T(1,128)S(1)}, s32[1,128]{1,0:T(1,128)}, u32[]{:S(2)}) copy-start(s32[1,128]{1,0:T(1,128)} %param.17) | copy-start | bytes 1540
  7.2 178.5 %all-gather.8.cloned.1.call-start = ((), (), s32[]{:S(2)}) async-start(), calls=%async_computation.2 | async-start | bytes 4456448 | tf_op jit(solution)/shard_map/all_gather | solution.py:195
  8.0 217.1 %all-gather.10.cloned.1.call-start = ((), (), s32[]{:S(2)}) async-start(), calls=%async_computation.3 | async-start | bytes 4456448 | tf_op jit(solution)/shard_map/all_gather | solution.py:194
  8.7 342.4 %all-gather.12.cloned.1.call-start = ((), (), s32[]{:S(2)}) async-start(), calls=%async_computation.4 | async-start | bytes 8912896 | tf_op jit(solution)/shard_map/all_gather | solution.py:193
  9.5 383.1 %all-gather.14.cloned.1.call-start = ((), (), s32[]{:S(2)}) async-start(), calls=%async_computation.5 | async-start | bytes 8912896 | tf_op jit(solution)/shard_map/all_gather | solution.py:214
  10.0 512.6 %all-gather.16.cloned.1.call-start = ((), (), s32[]{:S(2)}) async-start(), calls=%async_computation.6 | async-start | bytes 26738688 | tf_op jit(solution)/shard_map/all_gather | solution.py:218
  10.6 642.1 %all-gather.18.cloned.1.call-start = ((), (), s32[]{:S(2)}) async-start(), calls=%async_computation.7 | async-start | bytes 26738688 | tf_op jit(solution)/shard_map/all_gather | solution.py:225
  11.2 771.7 %all-gather.20.cloned.1.call-start = ((), (), s32[]{:S(2)}) async-start(), calls=%async_computation.8 | async-start | bytes 26738688 | tf_op jit(solution)/shard_map/all_gather | solution.py:238
  12.0 1342.9 %reduce-scatter.3.cloned.1.call-start = ((), (), s32[]{:S(2)}) async-start(), calls=%async_computation.9 | async-start | bytes 53477376 | tf_op jit(solution)/shard_map/reduce_scatter | solution.py:291
  12.0 30.9 %collective-permute-start = (bf16[128,6144]{1,0:T(8,128)(2,1)S(1)}, bf16[128,6144]{1,0:T(8,128)(2,1)}, u32[]{:S(2)}, u32[]{:S(2)}) collective-permute-start(bf16[128,6144]{1,0:T(8,128)(2,1)S(1)} %copy-done.17), channel_id=1, source_target_pairs={{0,1},{1,2},{2,3},{3,4},{4,5},{5,6},{6,7},{7,8},{8,9},{9,10},{10,1... | collective-permute-start | bytes 4718600 | tf_op jit(solution)/shard_map/ppermute | solution.py:20
  12.5 44.0 %collective-permute-start.1 = (bf16[128,6144]{1,0:T(8,128)(2,1)S(1)}, bf16[128,6144]{1,0:T(8,128)(2,1)}, u32[]{:S(2)}, u32[]{:S(2)}) collective-permute-start(bf16[128,6144]{1,0:T(8,128)(2,1)S(1)} %copy-done.17), channel_id=1, source_target_pairs={{0,15},{1,0},{2,1},{3,2},{4,3},{5,4},{6,5},{7,6},{8,7},{9,8},{10,9... | collective-permute-start | bytes 4718600 | tf_op jit(solution)/shard_map/ppermute | solution.py:23
  43.0 32.8 %collective-permute-start.2 = (bf16[128,6144]{1,0:T(8,128)(2,1)}, bf16[128,6144]{1,0:T(8,128)(2,1)S(1)}, u32[]{:S(2)}, u32[]{:S(2)}) collective-permute-start(bf16[128,6144]{1,0:T(8,128)(2,1)} %collective-permute-done), channel_id=1, source_target_pairs={{0,1},{1,2},{2,3},{3,4},{4,5},{5,6},{6,7},{7,8},{8,9},{9,10},{10,1... | collective-permute-start | bytes 4718600 | tf_op jit(solution)/shard_map/ppermute | solution.py:20
  56.6 40.7 %collective-permute-start.3 = (bf16[128,6144]{1,0:T(8,128)(2,1)}, bf16[128,6144]{1,0:T(8,128)(2,1)S(1)}, u32[]{:S(2)}, u32[]{:S(2)}) collective-permute-start(bf16[128,6144]{1,0:T(8,128)(2,1)} %collective-permute-done.1), channel_id=1, source_target_pairs={{0,15},{1,0},{2,1},{3,2},{4,3},{5,4},{6,5},{7,6},{8,7},{9,8},{10,9... | collective-permute-start | bytes 4718600 | tf_op jit(solution)/shard_map/ppermute | solution.py:23
  56.6 294.5 %copy-start.49 = (f32[128]{0:T(128)}, f32[128]{0:T(128)S(1)}, u32[]{:S(2)}) copy-start(f32[128]{0:T(128)S(1)} %add_rsqrt_fusion.3) | copy-start | bytes 1540
  75.8 43.0 %collective-permute-start.4 = (bf16[128,6144]{1,0:T(8,128)(2,1)S(1)}, bf16[128,6144]{1,0:T(8,128)(2,1)S(1)}, u32[]{:S(2)}, u32[]{:S(2)}) collective-permute-start(bf16[128,6144]{1,0:T(8,128)(2,1)S(1)} %collective-permute-done.2), channel_id=1, source_target_pairs={{0,1},{1,2},{2,3},{3,4},{4,5},{5,6},{6,7},{7,8},{8,9},{9,10},{10,1... | collective-permute-start | bytes 4718600 | tf_op jit(solution)/shard_map/ppermute | solution.py:20
  97.2 48.2 %collective-permute-start.5 = (bf16[128,6144]{1,0:T(8,128)(2,1)S(1)}, bf16[128,6144]{1,0:T(8,128)(2,1)S(1)}, u32[]{:S(2)}, u32[]{:S(2)}) collective-permute-start(bf16[128,6144]{1,0:T(8,128)(2,1)S(1)} %collective-permute-done.3), channel_id=1, source_target_pairs={{0,15},{1,0},{2,1},{3,2},{4,3},{5,4},{6,5},{7,6},{8,7},{9,8},{10,9... | collective-permute-start | bytes 4718600 | tf_op jit(solution)/shard_map/ppermute | solution.py:23
  118.8 47.8 %collective-permute-start.6 = (bf16[128,6144]{1,0:T(8,128)(2,1)S(1)}, bf16[128,6144]{1,0:T(8,128)(2,1)}, u32[]{:S(2)}, u32[]{:S(2)}) collective-permute-start(bf16[128,6144]{1,0:T(8,128)(2,1)S(1)} %collective-permute-done.4), channel_id=1, source_target_pairs={{0,1},{1,2},{2,3},{3,4},{4,5},{5,6},{6,7},{7,8},{8,9},{9,10},{10,1... | collective-permute-start | bytes 4718600 | tf_op jit(solution)/shard_map/ppermute | solution.py:20
  145.4 36.3 %collective-permute-start.7 = (bf16[128,6144]{1,0:T(8,128)(2,1)S(1)}, bf16[128,6144]{1,0:T(8,128)(2,1)S(1)}, u32[]{:S(2)}, u32[]{:S(2)}) collective-permute-start(bf16[128,6144]{1,0:T(8,128)(2,1)S(1)} %collective-permute-done.5), channel_id=1, source_target_pairs={{0,15},{1,0},{2,1},{3,2},{4,3},{5,4},{6,5},{7,6},{8,7},{9,8},{10,9... | collective-permute-start | bytes 4718600 | tf_op jit(solution)/shard_map/ppermute | solution.py:23
  148.0 37.8 %copy-start.41 = (f32[2048]{0:T(1024)S(1)}, f32[2048]{0:T(1024)}, u32[]{:S(2)}) copy-start(f32[2048]{0:T(1024)} %param.19) | copy-start | bytes 24580
  166.5 37.2 %collective-permute-start.8 = (bf16[128,6144]{1,0:T(8,128)(2,1)}, bf16[128,6144]{1,0:T(8,128)(2,1)}, u32[]{:S(2)}, u32[]{:S(2)}) collective-permute-start(bf16[128,6144]{1,0:T(8,128)(2,1)} %collective-permute-done.6), channel_id=1, source_target_pairs={{0,1},{1,2},{2,3},{3,4},{4,5},{5,6},{6,7},{7,8},{8,9},{9,10},{10,1... | collective-permute-start | bytes 4718600 | tf_op jit(solution)/shard_map/ppermute | solution.py:20
  181.7 47.5 %collective-permute-start.9 = (bf16[128,6144]{1,0:T(8,128)(2,1)S(1)}, bf16[128,6144]{1,0:T(8,128)(2,1)}, u32[]{:S(2)}, u32[]{:S(2)}) collective-permute-start(bf16[128,6144]{1,0:T(8,128)(2,1)S(1)} %collective-permute-done.7), channel_id=1, source_target_pairs={{0,15},{1,0},{2,1},{3,2},{4,3},{5,4},{6,5},{7,6},{8,7},{9,8},{10,9... | collective-permute-start | bytes 4718600 | tf_op jit(solution)/shard_map/ppermute | solution.py:23
  203.7 57.7 %collective-permute-start.10 = (bf16[128,6144]{1,0:T(8,128)(2,1)}, bf16[128,6144]{1,0:T(8,128)(2,1)}, u32[]{:S(2)}, u32[]{:S(2)}) collective-permute-start(bf16[128,6144]{1,0:T(8,128)(2,1)} %collective-permute-done.8), channel_id=1, source_target_pairs={{0,1},{1,2},{2,3},{3,4},{4,5},{5,6},{6,7},{7,8},{8,9},{9,10},{10,1... | collective-permute-start | bytes 4718600 | tf_op jit(solution)/shard_map/ppermute | solution.py:20
  228.4 51.2 %copy-start.47 = (f32[128,8]{0,1:T(8,128)}, f32[128,8]{0,1:T(8,128)S(1)}, u32[]{:S(2)}) copy-start(f32[128,8]{0,1:T(8,128)S(1)} %add_rsqrt_fusion.1) | copy-start | bytes 12292
  229.2 53.6 %collective-permute-start.11 = (bf16[128,6144]{1,0:T(8,128)(2,1)}, bf16[128,6144]{1,0:T(8,128)(2,1)S(1)}, u32[]{:S(2)}, u32[]{:S(2)}) collective-permute-start(bf16[128,6144]{1,0:T(8,128)(2,1)} %collective-permute-done.9), channel_id=1, source_target_pairs={{0,15},{1,0},{2,1},{3,2},{4,3},{5,4},{6,5},{7,6},{8,7},{9,8},{10,9... | collective-permute-start | bytes 4718600 | tf_op jit(solution)/shard_map/ppermute | solution.py:23
  261.5 44.8 %collective-permute-start.12 = (bf16[128,6144]{1,0:T(8,128)(2,1)}, bf16[128,6144]{1,0:T(8,128)(2,1)S(1)}, u32[]{:S(2)}, u32[]{:S(2)}) collective-permute-start(bf16[128,6144]{1,0:T(8,128)(2,1)} %collective-permute-done.10), channel_id=1, source_target_pairs={{0,1},{1,2},{2,3},{3,4},{4,5},{5,6},{6,7},{7,8},{8,9},{9,10},{10,1... | collective-permute-start | bytes 4718600 | tf_op jit(solution)/shard_map/ppermute | solution.py:20
  279.9 79.5 %copy-start.32 = (bf16[128,8,64]{2,0,1:T(8,128)(2,1)}, bf16[128,8,64]{2,0,1:T(8,128)(2,1)S(1)}, u32[]{:S(2)}) copy-start(bf16[128,8,64]{2,0,1:T(8,128)(2,1)S(1)} %get-tuple-element.50) | copy-start | bytes 393220
  282.8 36.6 %collective-permute-start.13 = (bf16[128,6144]{1,0:T(8,128)(2,1)S(1)}, bf16[128,6144]{1,0:T(8,128)(2,1)S(1)}, u32[]{:S(2)}, u32[]{:S(2)}) collective-permute-start(bf16[128,6144]{1,0:T(8,128)(2,1)S(1)} %collective-permute-done.11), channel_id=1, source_target_pairs={{0,15},{1,0},{2,1},{3,2},{4,3},{5,4},{6,5},{7,6},{8,7},{9,8},{10,9... | collective-permute-start | bytes 4718600 | tf_op jit(solution)/shard_map/ppermute | solution.py:23
  306.3 43.6 %collective-permute-start.14 = (bf16[128,6144]{1,0:T(8,128)(2,1)S(1)}, bf16[128,6144]{1,0:T(8,128)(2,1)S(1)}, u32[]{:S(2)}, u32[]{:S(2)}) collective-permute-start(bf16[128,6144]{1,0:T(8,128)(2,1)S(1)} %collective-permute-done.12), channel_id=1, source_target_pairs={{0,1},{1,2},{2,3},{3,4},{4,5},{5,6},{6,7},{7,8},{8,9},{9,10},{10,1... | collective-permute-start | bytes 4718600 | tf_op jit(solution)/shard_map/ppermute | solution.py:20
  359.2 33.4 %copy-start.22 = (bf16[128,16,64]{2,0,1:T(8,128)(2,1)}, bf16[128,16,64]{2,0,1:T(8,128)(2,1)S(1)}, u32[]{:S(2)}) copy-start(bf16[128,16,64]{2,0,1:T(8,128)(2,1)S(1)} %copy.126) | copy-start | bytes 786436
  359.4 33.2 %copy-start.24 = (bf16[128,16,64]{2,0,1:T(8,128)(2,1)}, bf16[128,16,64]{2,0,1:T(8,128)(2,1)S(1)}, u32[]{:S(2)}) copy-start(bf16[128,16,64]{2,0,1:T(8,128)(2,1)S(1)} %copy.127) | copy-start | bytes 786436
  361.4 37.6 %copy-start.27 = (bf16[8,128,2,128]{3,1,2,0:T(8,128)(2,1)}, bf16[8,128,2,128]{3,1,2,0:T(8,128)(2,1)S(1)}, u32[]{:S(2)}) copy-start(bf16[8,128,2,128]{3,1,2,0:T(8,128)(2,1)S(1)} %convolution_convert_fusion.1) | copy-start | bytes 1572868
  399.0 399.8 %copy-start.2 = (f32[128,2048]{1,0:T(8,128)}, f32[128,2048]{1,0:T(8,128)S(1)}, u32[]{:S(2)}) copy-start(f32[128,2048]{1,0:T(8,128)S(1)} %get-tuple-element.56) | copy-start | bytes 3145732
  399.9 263.9 %copy-start.18 = (bf16[128,2048]{1,0:T(8,128)(2,1)}, bf16[128,2048]{1,0:T(8,128)(2,1)S(1)}, u32[]{:S(2)}) copy-start(bf16[128,2048]{1,0:T(8,128)(2,1)S(1)} %multiply_convert_fusion.3) | copy-start | bytes 1572868
  399.9 252.9 %copy-start.19 = (bf16[128,2048]{1,0:T(8,128)(2,1)S(1)}, bf16[128,2048]{1,0:T(8,128)(2,1)}, u32[]{:S(2)}) copy-start(bf16[128,2048]{1,0:T(8,128)(2,1)} %param.16) | copy-start | bytes 1572868
  652.7 11.1 copy-start.29
  800.5 17.2 copy-start.4
  800.5 11.8 copy-start.10
  800.5 11.8 copy-start.46
  836.8 16.4 copy-start.30
  839.7 13.6 copy-start.20
  886.9 1841.4 %reduce-scatter.5.cloned.1.call-start = ((), (), s32[]{:S(2)}) async-start(), calls=%async_computation.10 | async-start | bytes 160432128 | tf_op jit(solution)/shard_map/reduce_scatter | solution.py:245
  888.3 32.9 %copy-start.14 = (bf16[128,6144]{1,0:T(8,128)(2,1)S(1)}, bf16[128,6144]{1,0:T(8,128)(2,1)}, u32[]{:S(2)}) copy-start(bf16[128,6144]{1,0:T(8,128)(2,1)} %get-tuple-element.26) | copy-start | bytes 4718596
  1069.6 1819.5 %all-reduce.4.cloned.1.call-start = ((), (), s32[]{:S(2)}) async-start(), calls=%async_computation.11 | async-start | bytes 12582912 | tf_op jit(solution)/shard_map/psum | solution.py:305
  2744.6 42.9 %copy-start.5 = (f32[128,2048]{1,0:T(8,128)S(1)}, f32[128,2048]{1,0:T(8,128)}, u32[]{:S(2)}) copy-start(f32[128,2048]{1,0:T(8,128)} %copy-done.4) | copy-start | bytes 3145732
  2744.7 45.5 %copy-start.3 = (f32[128,2048]{1,0:T(8,128)S(1)}, f32[128,2048]{1,0:T(8,128)}, u32[]{:S(2)}) copy-start(f32[128,2048]{1,0:T(8,128)} %copy-done.2) | copy-start | bytes 3145732
  (40 other events, 145.0 us)
Sparse Core Ops, SparseCore 0:
  10.2 81.3 all-gather.7
  93.8 82.4 all-gather.9
  178.4 111.1 all-gather.11
  291.6 100.9 all-gather.13
  394.1 128.5 all-gather.15
  524.1 128.5 all-gather.17
  654.3 128.5 all-gather.19
  887.0 467.7 reduce-scatter.2
  1359.1 1369.1 reduce-scatter.4
  2734.9 154.1 all-reduce.3
